TPU v7x, 32 devices: a whole 2x2x4 slice. The times are simulated.
32 devices in a mesh: row: 8 (over z, x), col: 4 (over y, core).
Axes of the slice: x: 2, y: 2, z: 4, core: 2. Of those that a mesh axis runs over, the one named last changes fastest.
Arguments:
- vectors: bfloat16 [4, 4, 8, 16, 256], P(None, 'col', 'row'), may hold values from -6 to 6
- tiles: bfloat16 [8, 4, 64, 256, 256], P('row', 'col'), may hold values from -0.0625 to 0.0625
- tile_coords: int32 [8, 4, 64, 2], P('row', 'col'), may hold values from 0 to 127, as said below
- tile_count: int32 [8, 4], P('row', 'col'), may hold values from 16 to 64, as said below
Outputs:
- product: float32 [4, 4, 8, 16, 256], P(None, 'col', 'row')
Inputs may be any that keep to these rules, and one draw needn't show every extreme that they name: `tile_coords`: for the device in grid row r and grid column c every slot's block row I has I % 8 == r, its block column J has (J // 8) % 4 == c, and J <= I. `tile_count`: counts differ from device to device; in every draw some device uses all 64 slots and some other uses 64 // 4.
All inputs are finite; a program needn't handle non-finite values.
Results may differ from a plain program's by a relative error of at most 0.0003.
Values may be sent and summed in bfloat16 or wider, within the bound.
No kernel may reach another device: no remote copies, remote signals or barrier semaphores. Data moves between devices by JAX's collectives and lax.ppermute only.
A program may use at most 64 MiB of HBM per device.

v0:
```python
import jax
import jax.numpy as jnp
from jax import lax
from jax.sharding import PartitionSpec as P

TILE_GROUP = 8


def body(vectors, tiles, tile_coords, tile_count):
    grid_rows = lax.axis_size("row")
    grid_cols = lax.axis_size("col")
    repeats = vectors.shape[0]
    vec_count = vectors.shape[3]
    tile_width = vectors.shape[4]
    slot_count = tiles.shape[2]
    cells = grid_rows * grid_cols
    local_blocks = vectors.reshape(repeats, 1, vec_count, tile_width)
    column_blocks = lax.all_gather(local_blocks, "row", axis=1, tiled=True).reshape(
        repeats * grid_rows, vec_count, tile_width
    )
    row_blocks = lax.all_gather(local_blocks, "col", axis=1, tiled=True).reshape(
        repeats * grid_cols, vec_count, tile_width
    )
    matrices_all = tiles.reshape(slot_count, tile_width, tile_width)
    coords_all = tile_coords.reshape(slot_count, 2)
    filled = tile_count.reshape(())
    turns = (filled + TILE_GROUP - 1) // TILE_GROUP
    row_slots = jnp.arange(repeats * grid_cols, dtype=jnp.int32)
    col_slots = jnp.arange(repeats * grid_rows, dtype=jnp.int32)
    group_ids = jnp.arange(TILE_GROUP, dtype=jnp.int32)

    def load_group(turn):
        start = turn * TILE_GROUP
        matrices = lax.dynamic_slice_in_dim(matrices_all, start, TILE_GROUP, 0)
        positions = lax.dynamic_slice_in_dim(coords_all, start, TILE_GROUP, 0)
        active = start + group_ids < filled
        upper_index = positions[:, 0] // cells * grid_cols + positions[:, 0] % cells // grid_rows
        lower_index = positions[:, 1] // cells * grid_rows + positions[:, 1] % grid_rows
        row_hits = jnp.where(
            active[:, None] & (upper_index[:, None] == row_slots[None, :]), 1.0, 0.0
        ).astype(jnp.float32)
        col_hits = jnp.where(
            active[:, None] & (lower_index[:, None] == col_slots[None, :]), 1.0, 0.0
        ).astype(jnp.float32)
        return (matrices, upper_index, lower_index, row_hits, col_hits)

    def forward_add(total, matrices, lower_index, row_hits):
        sources = jnp.take(column_blocks, lower_index, axis=0)
        terms = jnp.einsum("snb,smb->snm", sources, matrices, preferred_element_type=jnp.float32)
        return total + jnp.einsum("su,snm->unm", row_hits, terms, precision=lax.Precision.HIGHEST)

    def mirror_add(total, matrices, upper_index, col_hits):
        targets = jnp.take(row_blocks, upper_index, axis=0)
        terms = jnp.einsum("snb,sbm->snm", targets, matrices, preferred_element_type=jnp.float32)
        return total + jnp.einsum("sv,snm->vnm", col_hits, terms, precision=lax.Precision.HIGHEST)

    row_start = jnp.zeros((repeats * grid_cols, vec_count, tile_width), jnp.float32)
    col_start = jnp.zeros((repeats * grid_rows, vec_count, tile_width), jnp.float32)

    def forward_turn(turn, total):
        matrices, upper_index, lower_index, row_hits, col_hits = load_group(turn)
        return forward_add(total, matrices, lower_index, row_hits)

    def mirror_turn(turn, total):
        matrices, upper_index, lower_index, row_hits, col_hits = load_group(turn)
        return mirror_add(total, matrices, upper_index, col_hits)

    row_acc = lax.fori_loop(0, turns, forward_turn, row_start)
    col_acc = lax.fori_loop(0, turns, mirror_turn, col_start)
    row_terms = row_acc.reshape(repeats, grid_cols, vec_count, tile_width)
    col_terms = col_acc.reshape(repeats, grid_rows, vec_count, tile_width)
    row_whole = lax.psum(row_terms, "col")
    col_whole = lax.psum(col_terms, "row")
    row_mine = lax.dynamic_slice_in_dim(row_whole, lax.axis_index("col"), 1, 1)
    col_mine = lax.dynamic_slice_in_dim(col_whole, lax.axis_index("row"), 1, 1)
    return (row_mine + col_mine).reshape(repeats, 1, 1, vec_count, tile_width)


def solution(mesh):
    return jax.shard_map(
        body,
        mesh=mesh,
        in_specs=(
            P(None, "col", "row", None, None),
            P("row", "col", None, None, None),
            P("row", "col", None, None),
            P("row", "col"),
        ),
        out_specs=P(None, "col", "row", None, None),
        check_vma=False,
    )
```

profile of v0, /device:TPU:0, one launch (start us, length us, event | category | flops | bytes accessed | tf_op | source)
XLA Modules:
  0.0 193.9 jit_solution(9262916242494318244)
XLA Ops:
  6.5 0.0 copy-start
  6.5 0.0 all-reduce.3.cloned.1.call-start
  7.2 32.8 %all-gather = bf16[4,8,1,16,256]{4,3,2,1,0:T(8,128)(2,1)S(1)} all-gather(bf16[4,1,1,16,256]{4,3,2,1,0:T(8,128)(2,1)} %param.8), channel_id=2, replica_groups=mesh['row'=8,'col'=4] {'row'}, dimensions={1}, use_global_device_ids=true | all-gather | bytes 294912 | tf_op jit(solution)/shard_map/all_gather | solution.py:18
  40.0 16.9 %while.30 = (s32[]{:T(128)}, f32[16,16,256]{2,0,1:T(8,128)S(1)}, s32[]{:T(128)}, s32[]{:T(128)}, s32[64,2]{0,1:T(2,128)}, /*index=5*/bf16[32,16,256]{2,1,0:T(8,1...) while((s32[]{:T(128)}, f32[16,16,256]{2,0,1:T(8,128)S(1)}, ...), condition=%wide.region_1.2_spmd.clone, body=%wide.region_0.1_spmd.clone.sunk | while | flops 23168940 | bytes 2036267 | solution.py:68
  40.0 0.8 constant_dynamic-slice_fusion.4
  40.8 0.6 gather_fusion
  41.4 1.6 fusion.66
  43.0 0.7 fusion.67
  43.7 0.5 convolution_add_fusion.4
  44.3 0.8 constant_dynamic-slice_fusion.4
  45.0 0.6 gather_fusion
  45.6 1.6 fusion.66
  47.2 0.7 fusion.67
  47.9 0.5 convolution_add_fusion.4
  48.5 0.8 constant_dynamic-slice_fusion.4
  49.3 0.6 gather_fusion
  49.8 1.6 fusion.66
  51.5 0.7 fusion.67
  52.1 0.5 convolution_add_fusion.4
  52.7 0.8 constant_dynamic-slice_fusion.4
  53.5 0.6 gather_fusion
  54.0 1.6 fusion.66
  55.7 0.7 fusion.67
  56.3 0.5 convolution_add_fusion.4
  56.9 0.9 copy.5
  57.7 0.0 all-reduce.3.cloned.1.call-update
  57.8 0.0 all-reduce.5.cloned.1.call-start
  57.8 0.0 copy-done
  57.8 15.6 %all-gather.1 = bf16[4,4,1,16,256]{4,3,2,1,0:T(8,128)(2,1)S(1)} all-gather(bf16[4,1,1,16,256]{4,3,2,1,0:T(8,128)(2,1)S(1)} %copy-done), channel_id=3, replica_groups=mesh['row'=8,'col'=4] {'col'}, dimensions={1}, use_global_device_ids=true | all-gather | bytes 163840 | tf_op jit(solution)/shard_map/all_gather | solution.py:21
  73.5 17.5 %while.31 = (s32[]{:T(128)}, f32[32,16,256]{2,0,1:T(8,128)S(1)}, s32[]{:T(128)}, s32[]{:T(128)}, s32[64,2]{0,1:T(2,128)}, /*index=5*/bf16[16,16,256]{2,1,0:T(8,1...) while((s32[]{:T(128)}, f32[32,16,256]{2,0,1:T(8,128)S(1)}, ...), condition=%wide.region_4.5_spmd.clone, body=%wide.region_3.4_spmd.clone.sunk | while | flops 29526316 | bytes 2560555 | solution.py:69
  73.5 0.8 constant_dynamic-slice_fusion.5
  74.3 0.6 gather_fusion.1
  74.8 1.5 fusion.72
  76.4 0.7 fusion.74
  77.0 0.8 convolution_add_fusion.5
  77.9 0.8 constant_dynamic-slice_fusion.5
  78.7 0.6 gather_fusion.1
  79.2 1.5 fusion.72
  80.8 0.7 fusion.74
  81.4 0.8 convolution_add_fusion.5
  82.2 0.8 constant_dynamic-slice_fusion.5
  83.0 0.6 gather_fusion.1
  83.6 1.5 fusion.72
  85.1 0.7 fusion.74
  85.8 0.8 convolution_add_fusion.5
  86.6 0.8 constant_dynamic-slice_fusion.5
  87.4 0.6 gather_fusion.1
  88.0 1.5 fusion.72
  89.5 0.7 fusion.74
  90.2 0.8 convolution_add_fusion.5
  91.0 1.1 copy.6
  92.1 0.0 all-reduce.5.cloned.1.call-update
  92.1 11.5 %all-reduce.3.cloned.1.call-done = f32[4,4,16,256]{3,2,1,0:T(8,128)} async-done(((f32[4,4,16,256]{3,2,1,0:T(8,128)}), f32[4,4,16,256]{3,2,1,0:T(8,128)}) %all-reduce.3.cloned.1.call-update) | async-done | bytes 262160 | tf_op jit(solution)/shard_map/psum | solution.py:72
  103.6 82.0 %all-reduce.5.cloned.1.call-done = f32[4,8,16,256]{3,2,1,0:T(8,128)} async-done(((f32[4,8,16,256]{3,2,1,0:T(8,128)}), f32[4,8,16,256]{3,2,1,0:T(8,128)}) %all-reduce.5.cloned.1.call-update) | async-done | bytes 524304 | tf_op jit(solution)/shard_map/psum | solution.py:73
  185.6 1.5 add_bitcast_fusion.1
  (26 shorter events, 0.5 us)
Async XLA Ops:
  6.5 51.3 %copy-start = (bf16[4,1,1,16,256]{4,3,2,1,0:T(8,128)(2,1)S(1)}, bf16[4,1,1,16,256]{4,3,2,1,0:T(8,128)(2,1)}, u32[]{:S(2)}) copy-start(bf16[4,1,1,16,256]{4,3,2,1,0:T(8,128)(2,1)} %param.8) | copy-start | bytes 98308
  6.5 97.1 %all-reduce.3.cloned.1.call-start = ((), (), s32[]{:S(2)}) async-start(), calls=%async_computation | async-start | bytes 524288 | tf_op jit(solution)/shard_map/psum | solution.py:72
  57.8 127.8 %all-reduce.5.cloned.1.call-start = ((), (), s32[]{:S(2)}) async-start(), calls=%async_computation.1 | async-start | bytes 1048576 | tf_op jit(solution)/shard_map/psum | solution.py:73
Sparse Core Ops, SparseCore 0:
  57.9 45.6 all-reduce.2
  107.0 78.5 all-reduce.4
where the time goes:
time: 195 us; the launch traced here: 194 us
  waiting for transfers between devices  93.5 us (48%)
  blocking collectives  48.3 us (25%)
  matrix products  17.8 us (9%)
  between operations  14.1 us (7%)
  local copies, waits for them, and re-layouts  12.5 us (6%)
  other arithmetic  7.16 us (4%)
    psum x1, waiting for transfers between devices, body(): col_whole = lax.psum(col_terms, 'row')  82 us
    all_gather x1, blocking collectives, body(): lax.all_gather(local_blocks, 'row', axis=1, tiled=True)  32.8 us
    all_gather x1, blocking collectives, body(): lax.all_gather(local_blocks, 'col', axis=1, tiled=True)  15.6 us
    psum x1, waiting for transfers between devices, body(): row_whole = lax.psum(row_terms, 'col')  11.5 us
    dot_general x4, matrix products, forward_add(): jnp.einsum('snb,smb->snm', sources, matrices, preferred_element_type=jnp....  6.44 us
    dot_general x4, matrix products, mirror_add(): jnp.einsum('snb,sbm->snm', targets, matrices, preferred_element_type=jnp....  6.05 us
    dynamic_slice x8, local copies, waits for them, and re-layouts, load_group(): positions = lax.dynamic_slice_in_dim(coords_all, start, TILE_GROUP, 0)  6.04 us
    lt x8, other arithmetic, load_group(): active = start + group_ids < filled  5.23 us
  transfers between devices with their start and end apart: 2, of which 2 were waited for; matrix products, arithmetic and copies ran while one was open for 9% of the time, Pallas kernels for 0%

commit v1 on v0

--- a/solution.py
+++ b/solution.py
@@ -4,6 +4,12 @@
 from jax.sharding import PartitionSpec as P
 
 TILE_GROUP = 8
+
+
+def gather_from_all(x, axis, dim):
+    size = lax.axis_size(axis)
+    repeats = [size if d == dim else 1 for d in range(x.ndim)]
+    return lax.all_to_all(jnp.tile(x, repeats), axis, split_axis=dim, concat_axis=dim, tiled=True)
 
 
 def body(vectors, tiles, tile_coords, tile_count):
@@ -15,7 +21,7 @@
     slot_count = tiles.shape[2]
     cells = grid_rows * grid_cols
     local_blocks = vectors.reshape(repeats, 1, vec_count, tile_width)
-    column_blocks = lax.all_gather(local_blocks, "row", axis=1, tiled=True).reshape(
+    column_blocks = gather_from_all(local_blocks, "row", 1).reshape(
         repeats * grid_rows, vec_count, tile_width
     )
     row_blocks = lax.all_gather(local_blocks, "col", axis=1, tiled=True).reshape(

time: 195 us -> 174 us (0.89)
  blocking collectives: 48.3 us -> 5.63 us
  waiting for transfers between devices: 93.5 us -> 106 us
  starting transfers between devices: 0.04 us -> 7.36 us
    all_gather x1 -> x0, blocking collectives: 32.8 us -> none  [body(): lax.all_gather(local_blocks, 'row', axis=1, tiled=True)]
    psum x1, waiting for transfers between devices: 11.5 us -> 33.8 us  [body(): row_whole = lax.psum(row_terms, 'col')]
    all_gather x1, blocking collectives: 15.6 us -> 5.63 us  [body(): lax.all_gather(local_blocks, 'col', axis=1, tiled=True)]
    psum x1, waiting for transfers between devices: 82 us -> 72 us  [body(): col_whole = lax.psum(col_terms, 'row')]
    all_to_all x0 -> x1, starting transfers between devices: none -> 7.28 us  [gather_from_all(): lax.all_to_all(jnp.tile(x, repeats), axis, split_axis=dim, concat_axis=di...]
  transfers between devices with their start and end apart: 2 -> 3, of which waited for: 2 -> 2; matrix products, arithmetic and copies ran while one was open for 9% -> 21% of each run, Pallas kernels for 0% -> 0%
where the time goes in v1:
time: 174 us; the launch traced here: 172 us
  waiting for transfers between devices  106 us (61%)
  matrix products  17.8 us (10%)
  between operations  14.1 us (8%)
  local copies, waits for them, and re-layouts  14 us (8%)
  starting transfers between devices  7.36 us (4%)
  other arithmetic  7.16 us (4%)
  blocking collectives  5.63 us (3%)
    psum x1, waiting for transfers between devices, body(): col_whole = lax.psum(col_terms, 'row')  72 us
    psum x1, waiting for transfers between devices, body(): row_whole = lax.psum(row_terms, 'col')  33.8 us
    all_to_all x1, starting transfers between devices, gather_from_all(): lax.all_to_all(jnp.tile(x, repeats), axis, split_axis=dim, concat_axis=di...  7.28 us
    dot_general x4, matrix products, forward_add(): jnp.einsum('snb,smb->snm', sources, matrices, preferred_element_type=jnp....  6.44 us
    dot_general x4, matrix products, mirror_add(): jnp.einsum('snb,sbm->snm', targets, matrices, preferred_element_type=jnp....  6.04 us
    dynamic_slice x8, local copies, waits for them, and re-layouts, load_group(): positions = lax.dynamic_slice_in_dim(coords_all, start, TILE_GROUP, 0)  6.04 us
    all_gather x1, blocking collectives, body(): lax.all_gather(local_blocks, 'col', axis=1, tiled=True)  5.63 us
    lt x8, other arithmetic, load_group(): active = start + group_ids < filled  5.23 us
  transfers between devices with their start and end apart: 3, of which 2 were waited for; matrix products, arithmetic and copies ran while one was open for 21% of the time, Pallas kernels for 0%

profile of v1, /device:TPU:0, one launch (start us, length us, event | category | flops | bytes accessed | tf_op | source)
XLA Modules:
  0.0 172.4 jit_solution(2892209236763014326)
XLA Ops:
  6.5 1.5 tile.9
  8.0 7.3 %all-to-all-start = ((bf16[4,8,16,256]{3,2,0,1:T(8,128)(2,1)}), bf16[4,8,16,256]{3,2,0,1:T(8,128)(2,1)S(1)}, u32[]{:S(2)}, u32[]{:S(2)}) async-start(bf16[4,8,16,256]{3,2,0,1:T(8,128)(2,1)} %tile.9), calls=%async_computation | async-start | bytes 524288 | tf_op jit(solution)/shard_map/all_to_all | solution.py:12
  15.3 0.0 all-reduce.5.cloned.1.call-start
  16.0 5.6 %all-gather = bf16[4,4,1,16,256]{4,3,2,1,0:T(8,128)(2,1)S(1)} all-gather(bf16[4,1,1,16,256]{4,3,2,1,0:T(8,128)(2,1)} %param.8), channel_id=2, replica_groups=mesh['row'=8,'col'=4] {'col'}, dimensions={1}, use_global_device_ids=true | all-gather | bytes 163840 | tf_op jit(solution)/shard_map/all_gather | solution.py:27
  21.7 17.5 %while.31 = (s32[]{:T(128)}, f32[32,16,256]{2,0,1:T(8,128)S(1)}, s32[]{:T(128)}, s32[]{:T(128)}, s32[64,2]{0,1:T(2,128)}, /*index=5*/bf16[16,16,256]{2,1,0:T(8,1...) while((s32[]{:T(128)}, f32[32,16,256]{2,0,1:T(8,128)S(1)}, ...), condition=%wide.region_4.5_spmd.clone, body=%wide.region_3.4_spmd.clone.sunk | while | flops 29526316 | bytes 2560555 | solution.py:75
  21.7 0.8 constant_dynamic-slice_fusion.5
  22.5 0.6 gather_fusion.1
  23.1 1.5 fusion.72
  24.6 0.7 fusion.74
  25.3 0.8 convolution_add_fusion.5
  26.1 0.8 constant_dynamic-slice_fusion.5
  26.9 0.6 gather_fusion.1
  27.4 1.5 fusion.72
  29.0 0.7 fusion.74
  29.6 0.8 convolution_add_fusion.5
  30.4 0.8 constant_dynamic-slice_fusion.5
  31.2 0.6 gather_fusion.1
  31.8 1.5 fusion.72
  33.3 0.7 fusion.74
  34.0 0.8 convolution_add_fusion.5
  34.8 0.8 constant_dynamic-slice_fusion.5
  35.6 0.6 gather_fusion.1
  36.2 1.5 fusion.72
  37.7 0.7 fusion.74
  38.4 0.8 convolution_add_fusion.5
  39.2 1.1 copy.17
  40.3 0.0 all-reduce.5.cloned.1.call-update
  40.3 0.0 all-reduce.3.cloned.1.call-start
  40.3 0.0 all-to-all-done
  40.4 16.9 %while.30 = (s32[]{:T(128)}, f32[16,16,256]{2,0,1:T(8,128)S(1)}, s32[]{:T(128)}, s32[]{:T(128)}, s32[64,2]{0,1:T(2,128)}, /*index=5*/bf16[32,16,256]{2,1,0:T(8,1...) while((s32[]{:T(128)}, f32[16,16,256]{2,0,1:T(8,128)S(1)}, ...), condition=%wide.region_1.2_spmd.clone, body=%wide.region_0.1_spmd.clone.sunk | while | flops 23168940 | bytes 2036267 | solution.py:74
  40.4 0.8 constant_dynamic-slice_fusion.4
  41.2 0.6 gather_fusion
  41.8 1.6 fusion.66
  43.4 0.7 fusion.67
  44.1 0.5 convolution_add_fusion.4
  44.7 0.8 constant_dynamic-slice_fusion.4
  45.4 0.6 gather_fusion
  46.0 1.6 fusion.66
  47.6 0.7 fusion.67
  48.3 0.5 convolution_add_fusion.4
  48.9 0.8 constant_dynamic-slice_fusion.4
  49.7 0.6 gather_fusion
  50.2 1.6 fusion.66
  51.9 0.7 fusion.67
  52.5 0.5 convolution_add_fusion.4
  53.1 0.8 constant_dynamic-slice_fusion.4
  53.9 0.6 gather_fusion
  54.4 1.6 fusion.66
  56.1 0.7 fusion.67
  56.7 0.5 convolution_add_fusion.4
  57.3 0.9 copy.16
  58.1 0.0 all-reduce.3.cloned.1.call-update
  58.2 72.0 %all-reduce.5.cloned.1.call-done = f32[4,8,16,256]{3,2,1,0:T(8,128)} async-done(((f32[4,8,16,256]{3,2,1,0:T(8,128)}), f32[4,8,16,256]{3,2,1,0:T(8,128)}) %all-reduce.5.cloned.1.call-update) | async-done | bytes 524304 | tf_op jit(solution)/shard_map/psum | solution.py:79
  130.2 33.8 %all-reduce.3.cloned.1.call-done = f32[4,4,16,256]{3,2,1,0:T(8,128)} async-done(((f32[4,4,16,256]{3,2,1,0:T(8,128)}), f32[4,4,16,256]{3,2,1,0:T(8,128)}) %all-reduce.3.cloned.1.call-update) | async-done | bytes 262160 | tf_op jit(solution)/shard_map/psum | solution.py:78
  164.1 1.5 add_bitcast_fusion.1
  (27 shorter events, 0.5 us)
Async XLA Ops:
  8.0 32.3 %all-to-all-start = ((bf16[4,8,16,256]{3,2,0,1:T(8,128)(2,1)}), bf16[4,8,16,256]{3,2,0,1:T(8,128)(2,1)S(1)}, u32[]{:S(2)}, u32[]{:S(2)}) async-start(bf16[4,8,16,256]{3,2,0,1:T(8,128)(2,1)} %tile.9), calls=%async_computation | async-start | bytes 524288 | tf_op jit(solution)/shard_map/all_to_all | solution.py:12
  15.3 114.9 %all-reduce.5.cloned.1.call-start = ((), (), s32[]{:S(2)}) async-start(), calls=%async_computation.2 | async-start | bytes 1048576 | tf_op jit(solution)/shard_map/psum | solution.py:79
  40.3 123.8 %all-reduce.3.cloned.1.call-start = ((), (), s32[]{:S(2)}) async-start(), calls=%async_computation.1 | async-start | bytes 524288 | tf_op jit(solution)/shard_map/psum | solution.py:78
Sparse Core Ops, SparseCore 0:
  40.4 89.7 all-reduce.4
  132.5 31.4 all-reduce.2
